TPU v7x, 32 devices: a whole 2x2x4 slice. The times are simulated.
32 devices in a mesh: req: 16 (over z, y, x), tp: 2 (over core).
Axes of the slice: x: 2, y: 2, z: 4, core: 2. Of those that a mesh axis runs over, the one named last changes fastest.
Arguments:
- tokens: bfloat16 [2048, 2560], P('req'), may hold values from -6 to 6
- input_norm_gain: bfloat16 [2560], replicated, may hold values from 0.5 to 1.5
- query_weight: bfloat16 [2560, 4096], P(None, 'tp'), may hold values from -0.125 to 0.125
- key_value_weight: bfloat16 [2, 2560, 1024], P(None, None, 'tp'), may hold values from -0.125 to 0.125
- query_head_gain: bfloat16 [128], replicated, may hold values from 0.25 to 1.75
- key_head_gain: bfloat16 [128], replicated, may hold values from 0.25 to 1.75
- adapter_down_maps: bfloat16 [16, 48, 2560], P('req', None, 'tp'), may hold values from -0.125 to 0.125
- query_up_maps: bfloat16 [16, 16, 4096], P('req', None, 'tp'), may hold values from -0.75 to 0.75
- key_value_up_maps: bfloat16 [16, 2, 16, 1024], P('req', None, None, 'tp'), may hold values from -0.75 to 0.75
- packed_lengths: int32 [4], replicated, may hold values from 64 to 1024, as said below
- adapter_per_prompt: int32 [4], replicated, may hold values from 0 to 15, as said below
- adapter_place: int32 [16], replicated, may hold values from 0 to 15, each once
Outputs:
- attended: bfloat16 [2048, 4096], P('req', 'tp')
Inputs may be any that keep to these rules, and one draw needn't show every extreme that they name: `packed_lengths`: every entry is a multiple of 64; exactly one is 1024, at least one is 64, and they sum to 2048. `adapter_per_prompt`: the prompts use distinct adapters.
All inputs are finite; a program needn't handle non-finite values.
Results may differ from a plain program's by a relative error of at most 0.0086.
Values may be sent and summed in bfloat16 or wider, within the bound.
A program may use at most 128 MiB of HBM per device.

v0:
```python
import math
import jax
import jax.numpy as jnp
from jax import lax
from jax.sharding import PartitionSpec as P

SHORT_LEN = 64
epsilon = 1e-06
theta = 1000000.0
adapter_scale = 2.0


def normalize(values, gain_vec):
    values = values.astype(jnp.float32)
    inverse = lax.rsqrt(jnp.mean(values * values, axis=-1, keepdims=True) + epsilon)
    return values * inverse * gain_vec.astype(jnp.float32)


def rotate(values, offsets):
    half_dim = values.shape[-1] // 2
    powers = jnp.arange(half_dim, dtype=jnp.float32) * (2.0 / values.shape[-1])
    frequency = theta ** (-powers)
    angles = offsets.astype(jnp.float32)[:, None] * frequency[None, :]
    cosine = jnp.cos(angles)[:, None, :]
    sine_part = jnp.sin(angles)[:, None, :]
    former = values[..., :half_dim]
    latter = values[..., half_dim:]
    return jnp.concatenate(
        [former * cosine - latter * sine_part, latter * cosine + former * sine_part], axis=-1
    )


def doc_start(positions, packed_lengths):
    doc_end = jnp.cumsum(packed_lengths)
    return jnp.sum(
        jnp.where(doc_end[None, :] <= positions[:, None], packed_lengths[None, :], 0), axis=1
    )


def holders(positions, packed_lengths, adapter_per_prompt, adapter_place):
    doc_end = jnp.cumsum(packed_lengths)
    inside = (doc_end[None, :] > positions[:, None]) & (
        doc_end[None, :] - packed_lengths[None, :] <= positions[:, None]
    )
    adapter = jnp.sum(jnp.where(inside, adapter_per_prompt[None, :], 0), axis=1)
    catalog = jnp.arange(adapter_place.shape[0], dtype=jnp.int32)
    return jnp.sum(
        jnp.where(adapter[:, None] == catalog[None, :], adapter_place[None, :], 0), axis=1
    )


def on_device(
    tokens,
    input_norm_gain,
    query_weight,
    key_value_weight,
    query_head_gain,
    key_head_gain,
    adapter_down_maps,
    query_up_maps,
    key_value_up_maps,
    packed_lengths,
    adapter_per_prompt,
    adapter_place,
):
    token_rows = tokens.shape[0]
    first_row = lax.axis_index("req") * token_rows
    positions = first_row + jnp.arange(token_rows, dtype=jnp.int32)
    starts = doc_start(positions, packed_lengths)
    owners = holders(positions, packed_lengths, adapter_per_prompt, adapter_place)
    unit_count = token_rows // SHORT_LEN
    unit_owner = owners[::SHORT_LEN]
    normed = normalize(tokens, input_norm_gain).astype(jnp.bfloat16)
    plain_query = jnp.dot(normed, query_weight, preferred_element_type=jnp.float32)
    plain_pair = jnp.einsum(
        "td,cdk->ctk", normed, key_value_weight, preferred_element_type=jnp.float32
    )
    rank_width = query_up_maps.shape[1]
    local_width = adapter_down_maps.shape[2]
    own_cols = lax.dynamic_slice_in_dim(normed, lax.axis_index("tp") * local_width, local_width, 1)
    pieces = (
        lax.all_gather(adapter_down_maps, "req", axis=0, tiled=True),
        lax.all_gather(query_up_maps, "req", axis=0, tiled=True),
        lax.all_gather(key_value_up_maps, "req", axis=0, tiled=True),
    )
    piece_count = pieces[0].shape[0]
    slots_here = jnp.arange(piece_count, dtype=jnp.int32)
    chosen = (unit_owner[:, None] == slots_here[None, :]).astype(jnp.bfloat16)
    down_sel = jnp.einsum(
        "uk,krd->urd", chosen, pieces[0], preferred_element_type=jnp.float32
    ).astype(jnp.bfloat16)
    upq_sel = jnp.einsum(
        "uk,krc->urc", chosen, pieces[1], preferred_element_type=jnp.float32
    ).astype(jnp.bfloat16)
    upkv_sel = jnp.einsum(
        "uk,kcrd->ucrd", chosen, pieces[2], preferred_element_type=jnp.float32
    ).astype(jnp.bfloat16)
    partial_sum = jnp.einsum(
        "utd,urd->utr",
        own_cols.reshape(unit_count, SHORT_LEN, local_width),
        down_sel,
        preferred_element_type=jnp.float32,
    )
    reduced_rank = lax.psum(partial_sum, "tp").astype(jnp.bfloat16)
    query_increment = jnp.einsum(
        "utr,urc->utc", reduced_rank[..., :rank_width], upq_sel, preferred_element_type=jnp.float32
    ).reshape(token_rows, -1)
    pair_rank = reduced_rank[..., rank_width:].reshape(unit_count, SHORT_LEN, 2, rank_width)
    pair_increment = jnp.einsum(
        "utcr,ucrk->cutk", pair_rank, upkv_sel, preferred_element_type=jnp.float32
    ).reshape(2, token_rows, -1)
    head_width = query_head_gain.shape[0]
    query_heads = query_weight.shape[1] // head_width
    key_value_heads = key_value_weight.shape[2] // head_width
    group_width = query_heads // key_value_heads
    offsets = positions - starts
    query_rotated = (plain_query + adapter_scale * query_increment).reshape(
        token_rows, query_heads, head_width
    )
    query_rotated = rotate(normalize(query_rotated, query_head_gain), offsets).astype(jnp.bfloat16)
    query_every_token = query_rotated.reshape(token_rows, key_value_heads, group_width, head_width)
    key_rotated = (plain_pair[0] + adapter_scale * pair_increment[0]).reshape(
        token_rows, key_value_heads, head_width
    )
    key_rotated = rotate(normalize(key_rotated, key_head_gain), offsets).astype(jnp.bfloat16)
    value_every_token = (
        (plain_pair[1] + adapter_scale * pair_increment[1])
        .reshape(token_rows, key_value_heads, head_width)
        .astype(jnp.bfloat16)
    )
    key_value = jnp.stack([key_rotated, value_every_token], axis=1)
    start_sums = (
        jnp.zeros((token_rows, key_value_heads, group_width), jnp.float32),
        jnp.zeros((token_rows, key_value_heads, group_width, head_width), jnp.float32),
    )
    segment = lax.all_gather(key_value, "req", axis=0, tiled=True)
    length_now = segment.shape[0]
    key_rows = max(
        (size_try for size_try in range(1, min(length_now, 1024) + 1) if length_now % size_try == 0)
    )
    block_count = length_now // key_rows
    blocks = segment.reshape(block_count, key_rows, 2, key_value_heads, head_width)
    block_first = jnp.int32(0) + key_rows * jnp.arange(block_count, dtype=jnp.int32)

    def key_step(running, block_entry):
        key_block, block_start = block_entry
        key_pos = block_start + jnp.arange(key_rows, dtype=jnp.int32)
        key_start = doc_start(key_pos, packed_lengths)
        visible = (
            (key_start[None, :] == starts[:, None])
            & (key_pos[None, :] <= positions[:, None])
            & (key_pos[None, :] >= 0)
        )
        scores = jnp.einsum(
            "tkgd,skd->tkgs", query_every_token, key_block[:, 0], preferred_element_type=jnp.float32
        ) / math.sqrt(head_width)
        weights = jnp.where(visible[:, None, None, :], jnp.exp(scores), 0.0)
        totals = running[0] + jnp.sum(weights, axis=-1)
        numerator = running[1] + jnp.einsum(
            "tkgs,skd->tkgd",
            weights.astype(jnp.bfloat16),
            key_block[:, 1],
            preferred_element_type=jnp.float32,
        )
        return ((totals, numerator), None)

    result = lax.scan(key_step, start_sums, (blocks, block_first))[0]
    output_rows = result[1] / result[0][..., None]
    return output_rows.reshape(token_rows, query_heads * head_width).astype(jnp.bfloat16)


def solution(mesh):
    in_specs = (
        P("req", None),
        P(),
        P(None, "tp"),
        P(None, None, "tp"),
        P(),
        P(),
        P("req", None, "tp"),
        P("req", None, "tp"),
        P("req", None, None, "tp"),
        P(),
        P(),
        P(),
    )
    out_specs = P("req", "tp")
    return jax.shard_map(
        on_device, mesh=mesh, in_specs=in_specs, out_specs=out_specs, check_vma=False
    )
```

profile of v0, /device:TPU:0, one launch (start us, length us, event | category | flops | bytes accessed | tf_op | source)
XLA Modules:
  0.0 245.9 jit_solution(10807951525644673926)
XLA Ops:
  8.1 0.8 reduce-window.9
  9.6 46.1 %all_gather.13 = bf16[16,2,16,512]{3,2,1,0:T(8,128)(2,1)S(1)} all-gather(bf16[1,2,16,512]{3,2,1,0:T(8,128)(2,1)} %param.22), channel_id=1, replica_groups=mesh['req'=16,'tp'=2] {'req'}, dimensions={0}, use_global_device_ids=true | all-gather | bytes 557056 | tf_op jit(solution)/shard_map/all_gather | solution.py:84
  58.0 1.3 fusion.20
  59.3 1.3 fusion.22
  60.6 3.4 %convolution_bitcast_fusion = f32[2,128,512]{2,1,0:T(8,128)S(1)} fusion(bf16[2,2560,512]{2,1,0:T(8,128)(2,1)} %param.17, bf16[128,2560]{1,0:T(8,128)(2,1)S(1)} %fusion.22), kind=kOutput, calls=%fused_computation.33 | convolution fusion | flops 671088640 | bytes 6422528 | tf_op jit(solution)/shard_map/td,cdk->ctk/dot_general | solution.py:75
  65.0 8.9 %all-gather.4.cloned.1.call-done = bf16[16,48,1280]{2,1,0:T(8,128)(2,1)} async-done(((bf16[1,48,1280]{2,1,0:T(8,128)(2,1)}), bf16[16,48,1280]{2,1,0:T(8,128)(2,1)}) %all-gather.4.cloned.1.call-update) | async-done | bytes 1966096 | tf_op jit(solution)/shard_map/all_gather | solution.py:82
  74.0 2.3 convolution_convert_fusion
  76.4 3.7 %psum.7 = bf16[2,64,48]{1,2,0:T(8,128)(2,1)S(1)} all-reduce(f32[2,64,48]{1,2,0:T(8,128)S(1)} %fusion.27), channel_id=1, replica_groups=mesh['req'=16,'tp'=2] {'tp'}, use_global_device_ids=true, to_apply=%region_4.5 | all-reduce | flops 6144 | bytes 36864 | tf_op jit(solution)/shard_map/psum | solution.py:104
  81.2 0.8 pad_maximum_fusion.1
  82.2 48.5 %all-gather.8.cloned.1.call-done = bf16[16,16,2048]{2,1,0:T(8,128)(2,1)} async-done(((bf16[1,16,2048]{2,1,0:T(8,128)(2,1)}), bf16[16,16,2048]{2,1,0:T(8,128)(2,1)}) %all-gather.8.cloned.1.call-update) | async-done | bytes 1048592 | tf_op jit(solution)/shard_map/all_gather | solution.py:83
  130.7 2.4 convolution_convert_fusion.1
  133.5 5.5 %fusion.19 = f32[16,8,16,128]{3,1,2,0:T(8,128)S(1)} fusion(f32[128,2048]{1,0:T(8,128)S(1)} %bitcast.99, bf16[128,2560]{1,0:T(8,128)(2,1)S(1)} %fusion.22, bf16[2560,2048]{1,0:T(8,128)(2,1)} %param.16), kind=kOutput, calls=%fused_computation.29 | convolution fusion | flops 1342439424 | bytes 13238272 | tf_op jit(solution)/shard_map/dot_general | solution.py:74
  140.9 1.1 pad_maximum_fusion
  142.0 66.8 %all-gather.6.cloned.1.call-done = bf16[2048,2,4,128]{3,0,2,1:T(8,128)(2,1)} async-done(((bf16[128,2,4,128]{3,0,2,1:T(8,128)(2,1)}), bf16[2048,2,4,128]{3,0,2,1:T(8,128)(2,1)}) %all-gather.6.cloned.1.call-update) | async-done | bytes 4194320 | tf_op jit(solution)/shard_map/all_gather | solution.py:136
  208.8 29.5 %while.14 = (s32[]{:T(128)}, f32[128,4,4]{0,2,1:T(4,128)S(1)}, f32[128,4,4,128]{0,3,2,1:T(8,128)S(1)}, s32[1,4]{1,0:T(1,128)S(1)}, s32[2]{0:T(128)S(1)}, /*index...) while((s32[]{:T(128)}, f32[128,4,4]{0,2,1:T(4,128)S(1)}, ...), condition=%wide.region_12.13_spmd.clone, body=%wide.region_9.12_spmd.clone.sunk | while | flops 1087389824 | bytes 28237536 | solution.py:167
  210.9 0.9 and_and_fusion.2
  211.8 1.7 dynamic-slice_bitcast_fusion.2
  213.6 4.9 %fusion.54 = (f32[128,4,4]{0,2,1:T(4,128)S(1)}, f32[4,1024,128,4]{2,1,3,0:T(8,128)}) fusion(pred[128,1024]{0,1:T(8,128)(4,1)S(1)} %and_and_fusion.2, bf16[128,4,4,128]{3,0,2,1:T(8,128)(2,1)S(1)} %copy-done, bf16[1024,2,4,128]{3,0,2,1:T(8,128)(2,1)S(1)} %dynamic-slice_bitcast_fusion.2), kind=kOutput, calls=%fused_computation.3.clone.1 | convolution fusion | flops 543160320 | bytes 10100736 | tf_op jit(solution)/shard_map/while/body/eval_jaxpr/tkgd,skd->tkgs/dot_general | solution.py:154
  218.5 4.9 %fusion.55 = f32[128,4,4,128]{0,3,2,1:T(8,128)S(1)} fusion(f32[4,1024,128,4]{2,1,3,0:T(8,128)} %get-tuple-element.280, pred[128,1024]{0,1:T(8,128)(4,1)S(1)} %and_and_fusion.2, bf16[1024,2,4,128]{3,0,2,1:T(8,128)(2,1)S(1)} %dynamic-slice_bitcast_fusion.2, f32[128,4,4,128]{0,3,2,1:T(8,128)S(1)} %get-tuple-element.295, pred[]{:T(512)S(6)} %compare.3), kind=kOutput, calls=%fused_computation.10.clone.1 | convolution fusion | flops 543686656 | bytes 11665409 | tf_op jit(solution)/shard_map/while/body/eval_jaxpr/tkgs,skd->tkgd/dot_general | solution.py:159
  225.7 0.9 and_and_fusion.2
  226.6 1.7 dynamic-slice_bitcast_fusion.2
  228.3 4.9 %fusion.54 = (f32[128,4,4]{0,2,1:T(4,128)S(1)}, f32[4,1024,128,4]{2,1,3,0:T(8,128)}) fusion(pred[128,1024]{0,1:T(8,128)(4,1)S(1)} %and_and_fusion.2, bf16[128,4,4,128]{3,0,2,1:T(8,128)(2,1)S(1)} %copy-done, bf16[1024,2,4,128]{3,0,2,1:T(8,128)(2,1)S(1)} %dynamic-slice_bitcast_fusion.2), kind=kOutput, calls=%fused_computation.3.clone.1 | convolution fusion | flops 543160320 | bytes 10100736 | tf_op jit(solution)/shard_map/while/body/eval_jaxpr/tkgd,skd->tkgs/dot_general | solution.py:154
  233.3 4.9 %fusion.55 = f32[128,4,4,128]{0,3,2,1:T(8,128)S(1)} fusion(f32[4,1024,128,4]{2,1,3,0:T(8,128)} %get-tuple-element.280, pred[128,1024]{0,1:T(8,128)(4,1)S(1)} %and_and_fusion.2, bf16[1024,2,4,128]{3,0,2,1:T(8,128)(2,1)S(1)} %dynamic-slice_bitcast_fusion.2, f32[128,4,4,128]{0,3,2,1:T(8,128)S(1)} %get-tuple-element.295, pred[]{:T(512)S(6)} %compare.3), kind=kOutput, calls=%fused_computation.10.clone.1 | convolution fusion | flops 543686656 | bytes 11665409 | tf_op jit(solution)/shard_map/while/body/eval_jaxpr/tkgs,skd->tkgd/dot_general | solution.py:159
  238.4 1.0 copy.105
  (71 shorter events, 13.5 us)
Async XLA Ops:
  6.5 67.4 %all-gather.4.cloned.1.call-start = ((), (), s32[]{:S(2)}) async-start(), calls=%async_computation | async-start | bytes 2088960 | tf_op jit(solution)/shard_map/all_gather | solution.py:82
  7.3 123.4 %all-gather.8.cloned.1.call-start = ((), (), s32[]{:S(2)}) async-start(), calls=%async_computation.2 | async-start | bytes 1114112 | tf_op jit(solution)/shard_map/all_gather | solution.py:83
  8.0 200.8 %all-gather.6.cloned.1.call-start = ((), (), s32[]{:S(2)}) async-start(), calls=%async_computation.1 | async-start | bytes 4456448 | tf_op jit(solution)/shard_map/all_gather | solution.py:136
  60.6 3.5 %copy-start.2 = (bf16[128]{0:T(256)(128)(2,1)S(1)}, bf16[128]{0:T(256)(128)(2,1)}, u32[]{:S(2)}) copy-start(bf16[128]{0:T(256)(128)(2,1)} %param.19) | copy-start | bytes 772
  65.0 17.0 %copy-start.1 = (s32[4]{0:T(128)S(1)}, s32[4]{0:T(128)}, u32[]{:S(2)}) copy-start(s32[4]{0:T(128)} %param.23) | copy-start | bytes 52
  65.0 17.2 %copy-start.3 = (bf16[128]{0:T(256)(128)(2,1)S(1)}, bf16[128]{0:T(256)(128)(2,1)}, u32[]{:S(2)}) copy-start(bf16[128]{0:T(256)(128)(2,1)} %param.18) | copy-start | bytes 772
  208.8 4.8 %copy-start = (bf16[128,4,4,128]{3,0,2,1:T(8,128)(2,1)S(1)}, bf16[128,4,4,128]{3,0,2,1:T(8,128)(2,1)}, u32[]{:S(2)}) copy-start(bf16[128,4,4,128]{3,0,2,1:T(8,128)(2,1)} %get-tuple-element.313) | copy-start | bytes 1572868 | tf_op jit(solution)/shard_map/while
  223.5 4.8 %copy-start = (bf16[128,4,4,128]{3,0,2,1:T(8,128)(2,1)S(1)}, bf16[128,4,4,128]{3,0,2,1:T(8,128)(2,1)}, u32[]{:S(2)}) copy-start(bf16[128,4,4,128]{3,0,2,1:T(8,128)(2,1)} %get-tuple-element.313) | copy-start | bytes 1572868 | tf_op jit(solution)/shard_map/while
Sparse Core Ops, SparseCore 0:
  10.2 63.7 all-gather.3
  76.7 53.9 all-gather.7
  133.4 75.2 all-gather.5
where the time goes:
time: 247 us; the launch traced here: 246 us
  waiting for transfers between devices  126 us (51%)
  blocking collectives  49.8 us (20%)
  matrix products  34.5 us (14%)
  other arithmetic  15.3 us (6%)
  between operations  13.4 us (5%)
  local copies, waits for them, and re-layouts  7.03 us (3%)
    all_gather x1, waiting for transfers between devices, on_device(): segment = lax.all_gather(key_value, 'req', axis=0, tiled=True)  66.8 us
    all_gather x1, waiting for transfers between devices, on_device(): lax.all_gather(query_up_maps, 'req', axis=0, tiled=True)  48.5 us
    all_gather x1, blocking collectives, on_device(): lax.all_gather(key_value_up_maps, 'req', axis=0, tiled=True)  46.1 us
    dot_general x2, matrix products, key_step(): jnp.einsum('tkgs,skd->tkgd', weights.astype(jnp.bfloat16), key_block[:, 1...  9.88 us
    dot_general x2, matrix products, key_step(): jnp.einsum('tkgd,skd->tkgs', query_every_token, key_block[:, 0], preferre...  9.85 us
    all_gather x1, waiting for transfers between devices, on_device(): lax.all_gather(adapter_down_maps, 'req', axis=0, tiled=True)  8.92 us
    dot_general x1, matrix products, on_device(): jnp.dot(normed, query_weight, preferred_element_type=jnp.float32)  5.51 us
  transfers between devices with their start and end apart: 3, of which 3 were waited for; matrix products, arithmetic and copies ran while one was open for 11% of the time, Pallas kernels for 0%

commit v1 on v0

--- a/solution.py
+++ b/solution.py
@@ -8,6 +8,12 @@
 epsilon = 1e-06
 theta = 1000000.0
 adapter_scale = 2.0
+
+
+def drive_series_all(xs, axis_k):
+    outer = list(xs.shape[1:])
+    outer[axis_k] *= xs.shape[0]
+    return jnp.moveaxis(xs, 0, axis_k).reshape(outer)
 
 
 def normalize(values, gain_vec):
@@ -78,9 +84,30 @@
     rank_width = query_up_maps.shape[1]
     local_width = adapter_down_maps.shape[2]
     own_cols = lax.dynamic_slice_in_dim(normed, lax.axis_index("tp") * local_width, local_width, 1)
+
+    def state_threads_on_mesh(own_rows, axis_tag, axis_no):
+        many = jax.lax.axis_size(axis_tag)
+        store = tuple(((k0, (k0 + 1) % many) for k0 in range(many)))
+        bank = tuple(((rr, c) for c, rr in store))
+        raw_out, t1 = ([], [])
+        for kk in range(many - 1):
+            if kk % 2 == 0:
+                raw_out.append(
+                    jax.lax.ppermute(raw_out[-1] if raw_out else own_rows, axis_tag, store)
+                )
+            else:
+                back = jax.lax.ppermute(t1[-1] if t1 else own_rows, axis_tag, bank)
+                t1.append(back)
+        arr_now = jnp.stack([*raw_out[::-1], own_rows, *t1], axis=0)
+        b_now = jax.lax.axis_index(axis_tag)
+        local_part = len(raw_out)
+        shaped = b_now - local_part
+        arr_now = arr_now[(jnp.arange(many) - shaped) % many]
+        return drive_series_all(arr_now, axis_no)
+
     pieces = (
         lax.all_gather(adapter_down_maps, "req", axis=0, tiled=True),
-        lax.all_gather(query_up_maps, "req", axis=0, tiled=True),
+        state_threads_on_mesh(query_up_maps, axis_tag="req", axis_no=0),
         lax.all_gather(key_value_up_maps, "req", axis=0, tiled=True),
     )
     piece_count = pieces[0].shape[0]

time: 247 us -> 246 us (level)
  waiting for transfers between devices: 126 us -> 73.8 us
  starting transfers between devices: 0.08 us -> 42.2 us
  local copies, waits for them, and re-layouts: 7.03 us -> 14.5 us
  other arithmetic: 15.3 us -> 18.9 us
  blocking collectives: 49.8 us -> 46.3 us
    all_gather x1 -> x0, waiting for transfers between devices: 48.5 us -> none  [on_device(): lax.all_gather(query_up_maps, 'req', axis=0, tiled=True)]
    ppermute x0 -> x15, starting transfers between devices: none -> 42.1 us  [the longest x7 39.1 us: state_threads_on_mesh(): back = jax.lax.ppermute(t1[-1] if t1 else own_rows, axis_tag, bank)]
    ppermute x0 -> x15, waiting for transfers between devices: none -> 18 us  [the longest x8 13 us: state_threads_on_mesh(): jax.lax.ppermute(raw_out[-1] if raw_out else own_rows, axis_tag, store)]
    all_gather x1, waiting for transfers between devices: 66.8 us -> 55.8 us  [on_device(): segment = lax.all_gather(key_value, 'req', axis=0, tiled=True)]
    all_gather x1, waiting for transfers between devices: 8.92 us -> 0.02 us  [on_device(): lax.all_gather(adapter_down_maps, 'req', axis=0, tiled=True)]
    unnamed x7 -> x64, local copies, waits for them, and re-layouts: 0.21 us -> 6.27 us
    all_gather x1, blocking collectives: 46.1 us -> 42.4 us  [on_device(): lax.all_gather(key_value_up_maps, 'req', axis=0, tiled=True)]
  transfers between devices with their start and end apart: 3 -> 17, of which waited for: 3 -> 7; matrix products, arithmetic and copies ran while one was open for 11% -> 14% of each run, Pallas kernels for 0% -> 0%
where the time goes in v1:
time: 246 us; the launch traced here: 245 us
  waiting for transfers between devices  73.8 us (30%)
  blocking collectives  46.3 us (19%)
  starting transfers between devices  42.2 us (17%)
  matrix products  35.4 us (14%)
  other arithmetic  18.9 us (8%)
  local copies, waits for them, and re-layouts  14.5 us (6%)
  between operations  14 us (6%)
    all_gather x1, waiting for transfers between devices, on_device(): segment = lax.all_gather(key_value, 'req', axis=0, tiled=True)  55.8 us
    all_gather x1, blocking collectives, on_device(): lax.all_gather(key_value_up_maps, 'req', axis=0, tiled=True)  42.4 us
    ppermute x7, starting transfers between devices, state_threads_on_mesh(): back = jax.lax.ppermute(t1[-1] if t1 else own_rows, axis_tag, bank)  39.1 us
    ppermute x8, waiting for transfers between devices, state_threads_on_mesh(): jax.lax.ppermute(raw_out[-1] if raw_out else own_rows, axis_tag, store)  13 us
    dot_general x2, matrix products, key_step(): jnp.einsum('tkgs,skd->tkgd', weights.astype(jnp.bfloat16), key_block[:, 1...  11.8 us
    dot_general x2, matrix products, key_step(): jnp.einsum('tkgd,skd->tkgs', query_every_token, key_block[:, 0], preferre...  9.86 us
    unnamed x64, local copies, waits for them, and re-layouts  6.27 us
    dot_general x1, matrix products, on_device(): jnp.dot(normed, query_weight, preferred_element_type=jnp.float32)  5.54 us
  transfers between devices with their start and end apart: 17, of which 7 were waited for; matrix products, arithmetic and copies ran while one was open for 14% of the time, Pallas kernels for 0%

profile of v1, /device:TPU:0, one launch (start us, length us, event | category | flops | bytes accessed | tf_op | source)
XLA Modules:
  0.0 245.2 jit_solution(3321009628766194033)
XLA Ops:
  6.5 2.9 %collective-permute-start = (bf16[1,16,2048]{2,1,0:T(8,128)(2,1)}, bf16[1,16,2048]{2,1,0:T(8,128)(2,1)S(1)}, u32[]{:S(2)}, u32[]{:S(2)}) collective-permute-start(bf16[1,16,2048]{2,1,0:T(8,128)(2,1)} %param.21), channel_id=1, source_target_pairs={{0,2},{2,4},{4,6},{6,8},{8,10},{10,12},{12,14},{14,16},{16,18},{18... | collective-permute-start | bytes 196616 | tf_op jit(solution)/shard_map/ppermute | solution.py:96
  9.5 4.0 %collective-permute-start.8 = (bf16[1,16,2048]{2,1,0:T(8,128)(2,1)}, bf16[1,16,2048]{2,1,0:T(8,128)(2,1)S(1)}, u32[]{:S(2)}, u32[]{:S(2)}) collective-permute-start(bf16[1,16,2048]{2,1,0:T(8,128)(2,1)} %param.21), channel_id=1, source_target_pairs={{2,0},{4,2},{6,4},{8,6},{10,8},{12,10},{14,12},{16,14},{18,16},{20... | collective-permute-start | bytes 196616 | tf_op jit(solution)/shard_map/ppermute | solution.py:99
  20.0 3.5 %convolution_bitcast_fusion = f32[2,128,512]{2,1,0:T(8,128)S(1)} fusion(bf16[2,2560,512]{2,1,0:T(8,128)(2,1)} %param.17, bf16[128,2560]{1,0:T(8,128)(2,1)S(1)} %fusion.22), kind=kOutput, calls=%fused_computation.34 | convolution fusion | flops 671088640 | bytes 6422528 | tf_op jit(solution)/shard_map/td,cdk->ctk/dot_general | solution.py:81
  23.5 42.4 %all_gather.10 = bf16[16,2,16,512]{3,2,1,0:T(8,128)(2,1)S(1)} all-gather(bf16[1,2,16,512]{3,2,1,0:T(8,128)(2,1)S(1)} %copy-done.15), channel_id=1, replica_groups=mesh['req'=16,'tp'=2] {'req'}, dimensions={0}, use_global_device_ids=true | all-gather | bytes 557056 | tf_op jit(solution)/shard_map/all_gather | solution.py:111
  66.5 8.5 %collective-permute-done.1 = bf16[1,16,2048]{2,1,0:T(8,128)(2,1)S(1)} collective-permute-done((bf16[1,16,2048]{2,1,0:T(8,128)(2,1)S(1)}, bf16[1,16,2048]{2,1,0:T(8,128)(2,1)S(1)}, u32[]{:S(2)}, u32[]{:S(2)}) %collective-permute-start.1) | collective-permute-done | bytes 65568 | tf_op jit(solution)/shard_map/ppermute | solution.py:96
  75.0 5.7 %collective-permute-start.9 = (bf16[1,16,2048]{2,1,0:T(8,128)(2,1)S(1)}, bf16[1,16,2048]{2,1,0:T(8,128)(2,1)S(1)}, u32[]{:S(2)}, u32[]{:S(2)}) collective-permute-start(bf16[1,16,2048]{2,1,0:T(8,128)(2,1)S(1)} %collective-permute-done.8), channel_id=1, source_target_pairs={{2,0},{4,2},{6,4},{8,6},{10,8},{12,10},{14,12},{16,14},{18,16},{20... | collective-permute-start | bytes 196616 | tf_op jit(solution)/shard_map/ppermute | solution.py:99
  80.7 2.2 collective-permute-done.2
  83.0 5.7 %collective-permute-start.10 = (bf16[1,16,2048]{2,1,0:T(8,128)(2,1)S(1)}, bf16[1,16,2048]{2,1,0:T(8,128)(2,1)S(1)}, u32[]{:S(2)}, u32[]{:S(2)}) collective-permute-start(bf16[1,16,2048]{2,1,0:T(8,128)(2,1)S(1)} %collective-permute-done.9), channel_id=1, source_target_pairs={{2,0},{4,2},{6,4},{8,6},{10,8},{12,10},{14,12},{16,14},{18,16},{20... | collective-permute-start | bytes 196616 | tf_op jit(solution)/shard_map/ppermute | solution.py:99
  88.6 2.2 collective-permute-done.3
  93.2 5.6 %collective-permute-start.11 = (bf16[1,16,2048]{2,1,0:T(8,128)(2,1)S(1)}, bf16[1,16,2048]{2,1,0:T(8,128)(2,1)S(1)}, u32[]{:S(2)}, u32[]{:S(2)}) collective-permute-start(bf16[1,16,2048]{2,1,0:T(8,128)(2,1)S(1)} %collective-permute-done.10), channel_id=1, source_target_pairs={{2,0},{4,2},{6,4},{8,6},{10,8},{12,10},{14,12},{16,14},{18,16},{20... | collective-permute-start | bytes 196616 | tf_op jit(solution)/shard_map/ppermute | solution.py:99
  98.9 2.4 collective-permute-done.11
  101.2 6.1 %collective-permute-start.12 = (bf16[1,16,2048]{2,1,0:T(8,128)(2,1)S(1)}, bf16[1,16,2048]{2,1,0:T(8,128)(2,1)S(1)}, u32[]{:S(2)}, u32[]{:S(2)}) collective-permute-start(bf16[1,16,2048]{2,1,0:T(8,128)(2,1)S(1)} %collective-permute-done.11), channel_id=1, source_target_pairs={{2,0},{4,2},{6,4},{8,6},{10,8},{12,10},{14,12},{16,14},{18,16},{20... | collective-permute-start | bytes 196616 | tf_op jit(solution)/shard_map/ppermute | solution.py:99
  109.2 6.0 %collective-permute-start.13 = (bf16[1,16,2048]{2,1,0:T(8,128)(2,1)S(1)}, bf16[1,16,2048]{2,1,0:T(8,128)(2,1)}, u32[]{:S(2)}, u32[]{:S(2)}) collective-permute-start(bf16[1,16,2048]{2,1,0:T(8,128)(2,1)S(1)} %collective-permute-done.12), channel_id=1, source_target_pairs={{2,0},{4,2},{6,4},{8,6},{10,8},{12,10},{14,12},{16,14},{18,16},{20... | collective-permute-start | bytes 196616 | tf_op jit(solution)/shard_map/ppermute | solution.py:99
  117.1 6.1 %collective-permute-start.14 = (bf16[1,16,2048]{2,1,0:T(8,128)(2,1)}, bf16[1,16,2048]{2,1,0:T(8,128)(2,1)}, u32[]{:S(2)}, u32[]{:S(2)}) collective-permute-start(bf16[1,16,2048]{2,1,0:T(8,128)(2,1)} %collective-permute-done.13), channel_id=1, source_target_pairs={{2,0},{4,2},{6,4},{8,6},{10,8},{12,10},{14,12},{16,14},{18,16},{20... | collective-permute-start | bytes 196616 | tf_op jit(solution)/shard_map/ppermute | solution.py:99
  123.3 2.3 convolution_convert_fusion
  125.8 3.8 %psum.7 = bf16[2,64,48]{1,2,0:T(8,128)(2,1)S(1)} all-reduce(f32[2,64,48]{1,2,0:T(8,128)S(1)} %fusion.27), channel_id=1, replica_groups=mesh['req'=16,'tp'=2] {'tp'}, use_global_device_ids=true, to_apply=%region_4.5 | all-reduce | flops 6144 | bytes 36864 | tf_op jit(solution)/shard_map/psum | solution.py:131
  141.4 5.5 %fusion.19 = f32[16,8,16,128]{3,1,2,0:T(8,128)S(1)} fusion(f32[128,2048]{1,0:T(8,128)S(1)} %bitcast.134, bf16[128,2560]{1,0:T(8,128)(2,1)S(1)} %fusion.22, bf16[2560,2048]{1,0:T(8,128)(2,1)} %param.16), kind=kOutput, calls=%fused_computation.30 | convolution fusion | flops 1342439424 | bytes 13238272 | tf_op jit(solution)/shard_map/dot_general | solution.py:80
  149.2 55.8 %all-gather.5.cloned.1.call-done = bf16[2048,2,4,128]{3,0,2,1:T(8,128)(2,1)} async-done(((bf16[128,2,4,128]{3,0,2,1:T(8,128)(2,1)}), bf16[2048,2,4,128]{3,0,2,1:T(8,128)(2,1)}) %all-gather.5.cloned.1.call-update) | async-done | bytes 4194320 | tf_op jit(solution)/shard_map/all_gather | solution.py:163
  205.0 31.0 %while.14 = (s32[]{:T(128)}, f32[128,4,4]{0,2,1:T(4,128)S(1)}, f32[128,4,4,128]{0,3,2,1:T(8,128)}, s32[1,4]{1,0:T(1,128)S(1)}, s32[2]{0:T(128)S(1)}, /*index=5*/...) while((s32[]{:T(128)}, f32[128,4,4]{0,2,1:T(4,128)S(1)}, ...), condition=%wide.region_12.13_spmd.clone, body=%wide.region_9.12_spmd.clone.sunk | while | flops 1087389824 | bytes 26140356 | solution.py:194
  207.9 1.7 dynamic-slice_bitcast_fusion.2
  209.6 4.9 %fusion.56 = (f32[128,4,4]{0,2,1:T(4,128)S(1)}, f32[4,1024,128,4]{2,1,3,0:T(8,128)}) fusion(pred[128,1024]{0,1:T(8,128)(4,1)S(1)} %and_and_fusion.2, bf16[128,4,4,128]{3,0,2,1:T(8,128)(2,1)S(1)} %get-tuple-element.313, bf16[1024,2,4,128]{3,0,2,1:T(8,128)(2,1)S(1)} %dynamic-slice_bitcast_fusion.2), kind=kOutput, calls=%fused_computation.4.clone.1 | convolution fusion | flops 543160320 | bytes 10100736 | tf_op jit(solution)/shard_map/while/body/eval_jaxpr/tkgd,skd->tkgs/dot_general | solution.py:181
  214.6 5.8 %fusion.57 = f32[128,4,4,128]{0,3,2,1:T(8,128)} fusion(f32[4,1024,128,4]{2,1,3,0:T(8,128)} %get-tuple-element.280, pred[128,1024]{0,1:T(8,128)(4,1)S(1)} %and_and_fusion.2, bf16[1024,2,4,128]{3,0,2,1:T(8,128)(2,1)S(1)} %dynamic-slice_bitcast_fusion.2, f32[128,4,4,128]{0,3,2,1:T(8,128)} %get-tuple-element.295, pred[]{:T(512)S(6)} %compare.10), kind=kOutput, calls=%fused_computation.11.clone.1 | convolution fusion | flops 543686656 | bytes 11665409 | tf_op jit(solution)/shard_map/while/body/eval_jaxpr/tkgs,skd->tkgd/dot_general | solution.py:186
  225.0 4.9 %fusion.56 = (f32[128,4,4]{0,2,1:T(4,128)S(1)}, f32[4,1024,128,4]{2,1,3,0:T(8,128)}) fusion(pred[128,1024]{0,1:T(8,128)(4,1)S(1)} %and_and_fusion.2, bf16[128,4,4,128]{3,0,2,1:T(8,128)(2,1)S(1)} %get-tuple-element.313, bf16[1024,2,4,128]{3,0,2,1:T(8,128)(2,1)S(1)} %dynamic-slice_bitcast_fusion.2), kind=kOutput, calls=%fused_computation.4.clone.1 | convolution fusion | flops 543160320 | bytes 10100736 | tf_op jit(solution)/shard_map/while/body/eval_jaxpr/tkgd,skd->tkgs/dot_general | solution.py:181
  230.0 6.0 %fusion.57 = f32[128,4,4,128]{0,3,2,1:T(8,128)} fusion(f32[4,1024,128,4]{2,1,3,0:T(8,128)} %get-tuple-element.280, pred[128,1024]{0,1:T(8,128)(4,1)S(1)} %and_and_fusion.2, bf16[1024,2,4,128]{3,0,2,1:T(8,128)(2,1)S(1)} %dynamic-slice_bitcast_fusion.2, f32[128,4,4,128]{0,3,2,1:T(8,128)} %get-tuple-element.295, pred[]{:T(512)S(6)} %compare.10), kind=kOutput, calls=%fused_computation.11.clone.1 | convolution fusion | flops 543686656 | bytes 11665409 | tf_op jit(solution)/shard_map/while/body/eval_jaxpr/tkgs,skd->tkgd/dot_general | solution.py:186
  (155 shorter events, 37.0 us)
Async XLA Ops:
  6.5 116.8 %all-gather.3.cloned.1.call-start = ((), (), s32[]{:S(2)}) async-start(), calls=%async_computation | async-start | bytes 2088960 | tf_op jit(solution)/shard_map/all_gather | solution.py:109
  6.5 59.8 %collective-permute-start = (bf16[1,16,2048]{2,1,0:T(8,128)(2,1)}, bf16[1,16,2048]{2,1,0:T(8,128)(2,1)S(1)}, u32[]{:S(2)}, u32[]{:S(2)}) collective-permute-start(bf16[1,16,2048]{2,1,0:T(8,128)(2,1)} %param.21), channel_id=1, source_target_pairs={{0,2},{2,4},{4,6},{6,8},{8,10},{10,12},{12,14},{14,16},{16,18},{18... | collective-permute-start | bytes 196616 | tf_op jit(solution)/shard_map/ppermute | solution.py:96
  9.5 65.5 %collective-permute-start.8 = (bf16[1,16,2048]{2,1,0:T(8,128)(2,1)}, bf16[1,16,2048]{2,1,0:T(8,128)(2,1)S(1)}, u32[]{:S(2)}, u32[]{:S(2)}) collective-permute-start(bf16[1,16,2048]{2,1,0:T(8,128)(2,1)} %param.21), channel_id=1, source_target_pairs={{2,0},{4,2},{6,4},{8,6},{10,8},{12,10},{14,12},{16,14},{18,16},{20... | collective-permute-start | bytes 196616 | tf_op jit(solution)/shard_map/ppermute | solution.py:99
  13.5 191.5 %all-gather.5.cloned.1.call-start = ((), (), s32[]{:S(2)}) async-start(), calls=%async_computation.1 | async-start | bytes 4456448 | tf_op jit(solution)/shard_map/all_gather | solution.py:163
  20.0 103.3 %copy-start.18 = (s32[2]{0:T(128)}, s32[2]{0:T(128)S(1)}, u32[]{:S(2)}) copy-start(s32[2]{0:T(128)S(1)} %slice.44) | copy-start | bytes 28
  20.0 71.3 %copy-start.16 = (s32[4]{0:T(128)S(1)}, s32[4]{0:T(128)}, u32[]{:S(2)}) copy-start(s32[4]{0:T(128)} %param.23) | copy-start | bytes 52
  20.0 72.1 %copy-start.21 = (bf16[128]{0:T(256)(128)(2,1)S(1)}, bf16[128]{0:T(256)(128)(2,1)}, u32[]{:S(2)}) copy-start(bf16[128]{0:T(256)(128)(2,1)} %param.19) | copy-start | bytes 772
  20.0 72.7 %copy-start.22 = (bf16[128]{0:T(256)(128)(2,1)S(1)}, bf16[128]{0:T(256)(128)(2,1)}, u32[]{:S(2)}) copy-start(bf16[128]{0:T(256)(128)(2,1)} %param.18) | copy-start | bytes 772
  66.4 8.6 %collective-permute-start.1 = (bf16[1,16,2048]{2,1,0:T(8,128)(2,1)S(1)}, bf16[1,16,2048]{2,1,0:T(8,128)(2,1)S(1)}, u32[]{:S(2)}, u32[]{:S(2)}) collective-permute-start(bf16[1,16,2048]{2,1,0:T(8,128)(2,1)S(1)} %collective-permute-done), channel_id=1, source_target_pairs={{0,2},{2,4},{4,6},{6,8},{8,10},{10,12},{12,14},{14,16},{16,18},{18... | collective-permute-start | bytes 196616 | tf_op jit(solution)/shard_map/ppermute | solution.py:96
  75.0 7.9 %collective-permute-start.2 = (bf16[1,16,2048]{2,1,0:T(8,128)(2,1)S(1)}, bf16[1,16,2048]{2,1,0:T(8,128)(2,1)S(1)}, u32[]{:S(2)}, u32[]{:S(2)}) collective-permute-start(bf16[1,16,2048]{2,1,0:T(8,128)(2,1)S(1)} %collective-permute-done.1), channel_id=1, source_target_pairs={{0,2},{2,4},{4,6},{6,8},{8,10},{10,12},{12,14},{14,16},{16,18},{18... | collective-permute-start | bytes 196616 | tf_op jit(solution)/shard_map/ppermute | solution.py:96
  75.0 7.9 %collective-permute-start.9 = (bf16[1,16,2048]{2,1,0:T(8,128)(2,1)S(1)}, bf16[1,16,2048]{2,1,0:T(8,128)(2,1)S(1)}, u32[]{:S(2)}, u32[]{:S(2)}) collective-permute-start(bf16[1,16,2048]{2,1,0:T(8,128)(2,1)S(1)} %collective-permute-done.8), channel_id=1, source_target_pairs={{2,0},{4,2},{6,4},{8,6},{10,8},{12,10},{14,12},{16,14},{18,16},{20... | collective-permute-start | bytes 196616 | tf_op jit(solution)/shard_map/ppermute | solution.py:99
  82.9 8.0 %collective-permute-start.3 = (bf16[1,16,2048]{2,1,0:T(8,128)(2,1)S(1)}, bf16[1,16,2048]{2,1,0:T(8,128)(2,1)S(1)}, u32[]{:S(2)}, u32[]{:S(2)}) collective-permute-start(bf16[1,16,2048]{2,1,0:T(8,128)(2,1)S(1)} %collective-permute-done.2), channel_id=1, source_target_pairs={{0,2},{2,4},{4,6},{6,8},{8,10},{10,12},{12,14},{14,16},{16,18},{18... | collective-permute-start | bytes 196616 | tf_op jit(solution)/shard_map/ppermute | solution.py:96
  82.9 42.9 %copy-start.4 = (bf16[1,16,2048]{2,1,0:T(8,128)(2,1)}, bf16[1,16,2048]{2,1,0:T(8,128)(2,1)S(1)}, u32[]{:S(2)}) copy-start(bf16[1,16,2048]{2,1,0:T(8,128)(2,1)S(1)} %collective-permute-done.9) | copy-start | bytes 196612
  83.0 10.3 %collective-permute-start.10 = (bf16[1,16,2048]{2,1,0:T(8,128)(2,1)S(1)}, bf16[1,16,2048]{2,1,0:T(8,128)(2,1)S(1)}, u32[]{:S(2)}, u32[]{:S(2)}) collective-permute-start(bf16[1,16,2048]{2,1,0:T(8,128)(2,1)S(1)} %collective-permute-done.9), channel_id=1, source_target_pairs={{2,0},{4,2},{6,4},{8,6},{10,8},{12,10},{14,12},{16,14},{18,16},{20... | collective-permute-start | bytes 196616 | tf_op jit(solution)/shard_map/ppermute | solution.py:99
  90.9 8.0 %collective-permute-start.4 = (bf16[1,16,2048]{2,1,0:T(8,128)(2,1)S(1)}, bf16[1,16,2048]{2,1,0:T(8,128)(2,1)S(1)}, u32[]{:S(2)}, u32[]{:S(2)}) collective-permute-start(bf16[1,16,2048]{2,1,0:T(8,128)(2,1)S(1)} %collective-permute-done.3), channel_id=1, source_target_pairs={{0,2},{2,4},{4,6},{6,8},{8,10},{10,12},{12,14},{14,16},{16,18},{18... | collective-permute-start | bytes 196616 | tf_op jit(solution)/shard_map/ppermute | solution.py:96
  93.2 8.0 %collective-permute-start.11 = (bf16[1,16,2048]{2,1,0:T(8,128)(2,1)S(1)}, bf16[1,16,2048]{2,1,0:T(8,128)(2,1)S(1)}, u32[]{:S(2)}, u32[]{:S(2)}) collective-permute-start(bf16[1,16,2048]{2,1,0:T(8,128)(2,1)S(1)} %collective-permute-done.10), channel_id=1, source_target_pairs={{2,0},{4,2},{6,4},{8,6},{10,8},{12,10},{14,12},{16,14},{18,16},{20... | collective-permute-start | bytes 196616 | tf_op jit(solution)/shard_map/ppermute | solution.py:99
  98.8 8.5 %collective-permute-start.5 = (bf16[1,16,2048]{2,1,0:T(8,128)(2,1)S(1)}, bf16[1,16,2048]{2,1,0:T(8,128)(2,1)S(1)}, u32[]{:S(2)}, u32[]{:S(2)}) collective-permute-start(bf16[1,16,2048]{2,1,0:T(8,128)(2,1)S(1)} %collective-permute-done.4), channel_id=1, source_target_pairs={{0,2},{2,4},{4,6},{6,8},{8,10},{10,12},{12,14},{14,16},{16,18},{18... | collective-permute-start | bytes 196616 | tf_op jit(solution)/shard_map/ppermute | solution.py:96
  101.2 8.0 %collective-permute-start.12 = (bf16[1,16,2048]{2,1,0:T(8,128)(2,1)S(1)}, bf16[1,16,2048]{2,1,0:T(8,128)(2,1)S(1)}, u32[]{:S(2)}, u32[]{:S(2)}) collective-permute-start(bf16[1,16,2048]{2,1,0:T(8,128)(2,1)S(1)} %collective-permute-done.11), channel_id=1, source_target_pairs={{2,0},{4,2},{6,4},{8,6},{10,8},{12,10},{14,12},{16,14},{18,16},{20... | collective-permute-start | bytes 196616 | tf_op jit(solution)/shard_map/ppermute | solution.py:99
  107.3 7.9 %collective-permute-start.6 = (bf16[1,16,2048]{2,1,0:T(8,128)(2,1)S(1)}, bf16[1,16,2048]{2,1,0:T(8,128)(2,1)S(1)}, u32[]{:S(2)}, u32[]{:S(2)}) collective-permute-start(bf16[1,16,2048]{2,1,0:T(8,128)(2,1)S(1)} %collective-permute-done.5), channel_id=1, source_target_pairs={{0,2},{2,4},{4,6},{6,8},{8,10},{10,12},{12,14},{14,16},{16,18},{18... | collective-permute-start | bytes 196616 | tf_op jit(solution)/shard_map/ppermute | solution.py:96
  109.2 7.9 %collective-permute-start.13 = (bf16[1,16,2048]{2,1,0:T(8,128)(2,1)S(1)}, bf16[1,16,2048]{2,1,0:T(8,128)(2,1)}, u32[]{:S(2)}, u32[]{:S(2)}) collective-permute-start(bf16[1,16,2048]{2,1,0:T(8,128)(2,1)S(1)} %collective-permute-done.12), channel_id=1, source_target_pairs={{2,0},{4,2},{6,4},{8,6},{10,8},{12,10},{14,12},{16,14},{18,16},{20... | collective-permute-start | bytes 196616 | tf_op jit(solution)/shard_map/ppermute | solution.py:99
  115.2 8.0 %collective-permute-start.7 = (bf16[1,16,2048]{2,1,0:T(8,128)(2,1)S(1)}, bf16[1,16,2048]{2,1,0:T(8,128)(2,1)S(1)}, u32[]{:S(2)}, u32[]{:S(2)}) collective-permute-start(bf16[1,16,2048]{2,1,0:T(8,128)(2,1)S(1)} %collective-permute-done.6), channel_id=1, source_target_pairs={{0,2},{2,4},{4,6},{6,8},{8,10},{10,12},{12,14},{14,16},{16,18},{18... | collective-permute-start | bytes 196616 | tf_op jit(solution)/shard_map/ppermute | solution.py:96
  117.1 21.1 %collective-permute-start.14 = (bf16[1,16,2048]{2,1,0:T(8,128)(2,1)}, bf16[1,16,2048]{2,1,0:T(8,128)(2,1)}, u32[]{:S(2)}, u32[]{:S(2)}) collective-permute-start(bf16[1,16,2048]{2,1,0:T(8,128)(2,1)} %collective-permute-done.13), channel_id=1, source_target_pairs={{2,0},{4,2},{6,4},{8,6},{10,8},{12,10},{14,12},{16,14},{18,16},{20... | collective-permute-start | bytes 196616 | tf_op jit(solution)/shard_map/ppermute | solution.py:99
  147.7 57.3 %copy-start.17 = (s32[1,4]{1,0:T(1,128)S(1)}, s32[1,4]{1,0:T(1,128)}, u32[]{:S(2)}) copy-start(s32[1,4]{1,0:T(1,128)} %broadcast_in_dim.65) | copy-start | bytes 52
  147.7 57.3 %copy-start.23 = (s32[2]{0:T(128)S(1)}, s32[2]{0:T(128)}, u32[]{:S(2)}) copy-start(s32[2]{0:T(128)} %iota_multiply_fusion) | copy-start | bytes 28
  (17 other events, 261.7 us)
Sparse Core Ops, SparseCore 0:
  13.6 64.5 all-gather.2
  132.4 72.5 all-gather.4
